TPU v7x, 128 devices: a whole 4x4x4 slice. The times are simulated.
128 devices in a mesh: shards: 16 (over x, y), tensor: 4 (over z), section: 2 (over core).
Axes of the slice: x: 4, y: 4, z: 4, core: 2. Of those that a mesh axis runs over, the one named last changes fastest.
Arguments:
- gradient: bfloat16 [4, 768, 2048], P('section', 'tensor', 'shards'), may hold values from -36 to 36, as said below
- weight: bfloat16 [4, 768, 2048], P('section', 'tensor', 'shards'), may hold values from -0.21875 to 0.21875
- projector: float32 [4, 768, 256], P('section', 'tensor'), may hold values from -0.21875 to 0.21875
- first_moment: float32 [4, 256, 2048], P('section', 'tensor', 'shards'), may hold values from -0.3125 to 0.3125
- squared_moment: float32 [4, 256, 2048], P('section', 'tensor', 'shards'), may hold values from 1e-07 to 1e-05
- step_count: int32 [4], P('section'), may hold values from 1 to 11
- norm_gains: float32 [4, 768], P('section', 'tensor'), may hold values from 0.5 to 1.5
- gain_gradient: float32 [4, 768], P('section', 'tensor'), may hold values from -0.15625 to 0.15625
- gain_first: float32 [4, 768], P('section', 'tensor'), may hold values from -0.046875 to 0.046875
- gain_second: float32 [4, 768], P('section', 'tensor'), may hold values from 1e-08 to 1e-06
Outputs:
- weight_next: bfloat16 [4, 768, 2048], P('section', 'tensor', 'shards')
- fresh_projector: float32 [4, 768, 256], P('section', 'tensor')
- new_first: float32 [4, 256, 2048], P('section', 'tensor', 'shards')
- new_second: float32 [4, 256, 2048], P('section', 'tensor', 'shards')
- new_gains: float32 [4, 768], P('section', 'tensor')
- new_gain_first: float32 [4, 768], P('section', 'tensor')
- new_gain_second: float32 [4, 768], P('section', 'tensor')
Inputs may be any that keep to these rules, and one draw needn't show every extreme that they name: `gradient`: gradient entries are finite real numbers.
All inputs are finite; a program needn't handle non-finite values.
Results may differ from a plain program's by a relative error of at most 0.001.
Values sent between devices are 32-bit elements; how exact they have to be, the bound alone decides.
No kernel may reach another device: no remote copies, remote signals or barrier semaphores. Data moves between devices by JAX's collectives and lax.ppermute only.
A program may use at most 64 MiB of HBM per device.

v0:
```python
import jax
import jax.numpy as jnp
from jax import lax
from jax.sharding import PartitionSpec as P

NS_STEPS = 5
BETA_ONE = 0.9
BETA_TWO = 0.999
EPSILON = 1e-08
NORM_EPS = 1e-06
LEARN_RATE = 0.01
GALORE_SCALE = 0.25
WEIGHT_DECAY = 0.1


def newton_step(current, gram_matrix):
    return 1.5 * current - 0.5 * jnp.einsum(
        "mdr,mrs->mds", current, gram_matrix, precision=lax.Precision.HIGHEST
    )


def spread_orthogonalize(ranged):
    precision_highest = lax.Precision.HIGHEST
    squares = lax.psum(jnp.sum(ranged * ranged, axis=(1, 2)), ("shards", "tensor"))
    current = ranged / (jnp.sqrt(squares) + NORM_EPS)[:, None, None]
    for sweep_index in range(NS_STEPS):
        gram_matrix = lax.psum(
            jnp.einsum("mdr,mds->mrs", current, current, precision=precision_highest),
            ("shards", "tensor"),
        )
        current = newton_step(current, gram_matrix)
    return current


def shards(
    gradient,
    weight,
    projector,
    first_moment,
    squared_moment,
    step_count,
    norm_gains,
    gain_gradient,
    gain_first,
    gain_second,
):
    precision_highest = lax.Precision.HIGHEST
    gradient_widened = gradient.astype(jnp.float32)
    folded = lax.psum(
        jnp.einsum("mdf,mdr->mfr", gradient_widened, projector, precision=precision_highest),
        "tensor",
    )
    ranged_part = jnp.einsum("mdf,mfr->mdr", gradient_widened, folded, precision=precision_highest)
    ranged = lax.psum_scatter(ranged_part, "shards", scatter_dimension=1, tiled=True)
    fresh_projector = lax.all_gather(spread_orthogonalize(ranged), "shards", axis=1, tiled=True)
    projected_slice = jnp.einsum(
        "uqk,uqc->ukc", fresh_projector, gradient_widened, precision=precision_highest
    )
    own_rank = first_moment.shape[1]
    complete_rows = lax.psum(projected_slice, "tensor")
    projected = lax.dynamic_slice_in_dim(
        complete_rows, lax.axis_index("tensor") * own_rank, own_rank, 1
    )
    steps_float = step_count.astype(jnp.float32)[:, None, None]
    new_first = BETA_ONE * first_moment + (1.0 - BETA_ONE) * projected
    new_second = BETA_TWO * squared_moment + (1.0 - BETA_TWO) * projected * projected
    direction = (
        new_first
        / (1.0 - BETA_ONE**steps_float)
        / (jnp.sqrt(new_second / (1.0 - BETA_TWO**steps_float)) + EPSILON)
    )
    update = jnp.einsum(
        "hxp,hpq->hxq",
        fresh_projector,
        lax.all_gather(direction, "tensor", axis=1, tiled=True),
        precision=precision_highest,
    )
    weight_float = weight.astype(jnp.float32)
    weight_next = (
        weight_float - LEARN_RATE * (GALORE_SCALE * update + WEIGHT_DECAY * weight_float)
    ).astype(jnp.bfloat16)
    gain_steps = step_count.astype(jnp.float32)[:, None]
    new_gain_first = BETA_ONE * gain_first + (1.0 - BETA_ONE) * gain_gradient
    new_gain_second = BETA_TWO * gain_second + (1.0 - BETA_TWO) * gain_gradient * gain_gradient
    new_gains = norm_gains - LEARN_RATE * (new_gain_first / (1.0 - BETA_ONE**gain_steps)) / (
        jnp.sqrt(new_gain_second / (1.0 - BETA_TWO**gain_steps)) + EPSILON
    )
    return (
        weight_next,
        fresh_projector,
        new_first,
        new_second,
        new_gains,
        new_gain_first,
        new_gain_second,
    )


def solution(mesh):
    return jax.shard_map(
        shards,
        mesh=mesh,
        in_specs=(
            P("section", "tensor", "shards"),
            P("section", "tensor", "shards"),
            P("section", "tensor", None),
            P("section", "tensor", "shards"),
            P("section", "tensor", "shards"),
            P("section"),
            P("section", "tensor"),
            P("section", "tensor"),
            P("section", "tensor"),
            P("section", "tensor"),
        ),
        out_specs=(
            P("section", "tensor", "shards"),
            P("section", "tensor", None),
            P("section", "tensor", "shards"),
            P("section", "tensor", "shards"),
            P("section", "tensor"),
            P("section", "tensor"),
            P("section", "tensor"),
        ),
        check_vma=False,
    )
```

profile of v0, /device:TPU:0, one launch (start us, length us, event | category | flops | bytes accessed | tf_op | source)
XLA Modules:
  0.0 1052.9 jit_solution(11684637184179411351)
XLA Ops:
  7.2 0.0 copy-start
  7.2 0.0 all-reduce.10.cloned.1.call-start
  7.2 0.9 copy-done
  8.2 1.9 fusion.14
  10.1 0.0 copy-start.2
  10.1 0.0 all-reduce.10.cloned.1.call-update
  10.1 0.0 all-reduce.24.cloned.1.call-start
  10.2 45.4 %all-reduce.10.cloned.1.call-done = f32[2,128,256]{2,1,0:T(8,128)} async-done(((f32[2,128,256]{2,1,0:T(8,128)}), f32[2,128,256]{2,1,0:T(8,128)}) %all-reduce.10.cloned.1.call-update) | async-done | bytes 262160 | tf_op jit(solution)/shard_map/psum | solution.py:49
  55.5 0.0 copy-done.2
  55.6 1.3 convolution_bitcast_fusion
  56.8 1.1 copy.17
  57.9 0.0 all-reduce.24.cloned.1.call-update
  57.9 0.0 all-reduce.12.cloned.1.call-start
  58.0 0.0 copy-start.11
  58.0 0.6 copy-done.11
  58.6 0.6 dynamic-slice
  59.9 84.4 %all-reduce.24.cloned.1.call-done = f32[2,192,256]{2,0,1:T(2,128)} async-done(((f32[2,192,256]{2,0,1:T(2,128)}), f32[2,192,256]{2,0,1:T(2,128)}) %all-reduce.24.cloned.1.call-update) | async-done | bytes 393232
  144.2 0.9 multiply_reduce_fusion
  145.1 176.9 %psum.57 = f32[2]{0:T(128)S(1)} all-reduce(f32[2]{0:T(128)S(1)} %get-tuple-element.20), channel_id=1, replica_groups=mesh['shards'=16,'tensor'=4,'section'=2] {'shards','tensor'}, use_global_device_ids=true, to_apply=%region_3.0 | all-reduce | flops 2 | bytes 16 | tf_op jit(solution)/shard_map/psum | solution.py:24
  322.0 1.5 fusion.10
  323.5 0.0 all-reduce.12.cloned.1.call-update
  323.6 0.0 all-reduce.14.cloned.1.call-start
  323.6 121.5 %all-reduce.12.cloned.1.call-done = f32[2,256,256]{2,1,0:T(8,128)} async-done(((f32[2,256,256]{2,1,0:T(8,128)}), f32[2,256,256]{2,1,0:T(8,128)}) %all-reduce.12.cloned.1.call-update) | async-done | bytes 524304 | tf_op jit(solution)/shard_map/psum | solution.py:27
  445.1 1.4 fusion.8
  446.6 1.4 fusion.15
  448.0 0.0 all-reduce.14.cloned.1.call-update
  448.0 0.0 all-reduce.16.cloned.1.call-start
  448.0 127.3 %all-reduce.14.cloned.1.call-done = f32[2,256,256]{2,1,0:T(8,128)} async-done(((f32[2,256,256]{2,1,0:T(8,128)}), f32[2,256,256]{2,1,0:T(8,128)}) %all-reduce.14.cloned.1.call-update) | async-done | bytes 524304 | tf_op jit(solution)/shard_map/psum | solution.py:27
  575.3 1.4 fusion.7
  576.7 1.4 fusion.16
  578.1 0.0 all-reduce.16.cloned.1.call-update
  578.1 0.0 all-reduce.18.cloned.1.call-start
  578.2 127.2 %all-reduce.16.cloned.1.call-done = f32[2,256,256]{2,1,0:T(8,128)} async-done(((f32[2,256,256]{2,1,0:T(8,128)}), f32[2,256,256]{2,1,0:T(8,128)}) %all-reduce.16.cloned.1.call-update) | async-done | bytes 524304 | tf_op jit(solution)/shard_map/psum | solution.py:27
  705.4 1.4 fusion.6
  706.8 1.4 fusion.17
  708.3 0.0 all-reduce.18.cloned.1.call-update
  708.3 0.0 all-reduce.20.cloned.1.call-start
  708.3 127.3 %all-reduce.18.cloned.1.call-done = f32[2,256,256]{2,1,0:T(8,128)} async-done(((f32[2,256,256]{2,1,0:T(8,128)}), f32[2,256,256]{2,1,0:T(8,128)}) %all-reduce.18.cloned.1.call-update) | async-done | bytes 524304 | tf_op jit(solution)/shard_map/psum | solution.py:27
  835.6 1.4 fusion.5
  837.0 1.4 fusion.18
  838.4 0.0 all-reduce.20.cloned.1.call-update
  838.4 0.0 all-reduce.22.cloned.1.call-start
  838.5 127.4 %all-reduce.20.cloned.1.call-done = f32[2,256,256]{2,1,0:T(8,128)} async-done(((f32[2,256,256]{2,1,0:T(8,128)}), f32[2,256,256]{2,1,0:T(8,128)}) %all-reduce.20.cloned.1.call-update) | async-done | bytes 524304 | tf_op jit(solution)/shard_map/psum | solution.py:27
  965.9 1.4 fusion.4
  967.3 22.4 %all_gather.6 = f32[2,192,256]{2,0,1:T(2,128)S(1)} all-gather(f32[2,12,256]{2,0,1:T(2,128)S(1)} %copy.19), channel_id=1, replica_groups=mesh['shards'=16,'tensor'=4,'section'=2] {'shards'}, dimensions={1}, use_global_device_ids=true | all-gather | bytes 417792 | tf_op jit(solution)/shard_map/all_gather | solution.py:55
  989.8 0.0 copy-start.1
  989.8 1.4 fusion.19
  991.2 0.0 copy-start.5
  991.2 0.0 all-reduce.22.cloned.1.call-update
  991.2 0.6 copy-done.10
  991.8 0.0 copy-start.6
  991.8 0.0 copy-done.8
  991.8 0.0 copy-done.9
  991.9 0.6 copy-done.7
  992.5 0.0 copy-done.6
  992.5 0.7 divide_subtract_fusion
  993.2 37.8 %all-reduce.22.cloned.1.call-done = f32[2,256,128]{2,1,0:T(8,128)} async-done(((f32[2,256,128]{2,1,0:T(8,128)}), f32[2,256,128]{2,1,0:T(8,128)}) %all-reduce.22.cloned.1.call-update) | async-done | bytes 262160 | tf_op jit(solution)/shard_map/psum | solution.py:60
  1031.0 0.0 copy-done.4
  1031.0 0.0 copy-done.5
  1031.0 1.5 multiply_divide_fusion
  1032.5 12.4 %all_gather.7 = f32[2,256,128]{2,1,0:T(8,128)S(1)} all-gather(f32[2,64,128]{2,1,0:T(8,128)S(1)} %get-tuple-element.17), channel_id=1, replica_groups=mesh['shards'=16,'tensor'=4,'section'=2] {'tensor'}, dimensions={1}, use_global_device_ids=true | all-gather | bytes 327680 | tf_op jit(solution)/shard_map/all_gather | solution.py:75
  1044.9 0.0 copy-done.1
  1044.9 0.0 copy-done.3
  1044.9 1.2 fusion.3
  (10 shorter events, 0.1 us)
Async XLA Ops:
  7.2 1.0 copy-start
  7.2 48.4 %all-reduce.10.cloned.1.call-start = ((), (), s32[]{:S(2)}) async-start(), calls=%async_computation | async-start | bytes 524288 | tf_op jit(solution)/shard_map/psum | solution.py:49
  10.1 45.5 %copy-start.2 = (bf16[2,192,128]{2,1,0:T(8,128)(2,1)S(1)}, bf16[2,192,128]{2,1,0:T(8,128)(2,1)}, u32[]{:S(2)}) copy-start(bf16[2,192,128]{2,1,0:T(8,128)(2,1)} %param.10) | copy-start | bytes 294916
  10.1 134.1 %all-reduce.24.cloned.1.call-start = ((), (), s32[]{:S(2)}) async-start(), calls=%async_computation.7 | async-start | bytes 786432
  57.9 387.2 %all-reduce.12.cloned.1.call-start = ((), (), s32[]{:S(2)}) async-start(), calls=%async_computation.1 | async-start | bytes 1048576 | tf_op jit(solution)/shard_map/psum | solution.py:27
  58.0 0.7 copy-start.11
  323.6 251.7 %all-reduce.14.cloned.1.call-start = ((), (), s32[]{:S(2)}) async-start(), calls=%async_computation.2 | async-start | bytes 1048576 | tf_op jit(solution)/shard_map/psum | solution.py:27
  448.0 257.4 %all-reduce.16.cloned.1.call-start = ((), (), s32[]{:S(2)}) async-start(), calls=%async_computation.3 | async-start | bytes 1048576 | tf_op jit(solution)/shard_map/psum | solution.py:27
  578.1 257.4 %all-reduce.18.cloned.1.call-start = ((), (), s32[]{:S(2)}) async-start(), calls=%async_computation.4 | async-start | bytes 1048576 | tf_op jit(solution)/shard_map/psum | solution.py:27
  708.3 257.6 %all-reduce.20.cloned.1.call-start = ((), (), s32[]{:S(2)}) async-start(), calls=%async_computation.5 | async-start | bytes 1048576 | tf_op jit(solution)/shard_map/psum | solution.py:27
  838.4 192.5 %all-reduce.22.cloned.1.call-start = ((), (), s32[]{:S(2)}) async-start(), calls=%async_computation.6 | async-start | bytes 524288 | tf_op jit(solution)/shard_map/psum | solution.py:60
  989.8 55.1 %copy-start.1 = (f32[2,192,256]{2,1,0:T(8,128)}, f32[2,192,256]{2,1,0:T(8,128)S(1)}, u32[]{:S(2)}) copy-start(f32[2,192,256]{2,1,0:T(8,128)S(1)} %copy.21) | copy-start | bytes 1179652
  991.1 0.7 copy-start.10
  991.1 0.7 copy-start.8
  991.1 0.7 copy-start.9
  991.1 39.8 %copy-start.4 = (f32[2,64,128]{2,1,0:T(8,128)S(1)}, f32[2,64,128]{2,1,0:T(8,128)}, u32[]{:S(2)}) copy-start(f32[2,64,128]{2,1,0:T(8,128)} %param.14) | copy-start | bytes 196612
  991.2 39.8 %copy-start.5 = (f32[2,64,128]{2,1,0:T(8,128)S(1)}, f32[2,64,128]{2,1,0:T(8,128)}, u32[]{:S(2)}) copy-start(f32[2,64,128]{2,1,0:T(8,128)} %param.13) | copy-start | bytes 196612
  991.8 0.7 copy-start.7
  991.8 0.7 copy-start.6
  1032.5 12.4 %copy-start.3 = (bf16[2,192,128]{2,1,0:T(8,128)(2,1)S(1)}, bf16[2,192,128]{2,1,0:T(8,128)(2,1)}, u32[]{:S(2)}) copy-start(bf16[2,192,128]{2,1,0:T(8,128)(2,1)} %param.11) | copy-start | bytes 294916
Sparse Core Ops, SparseCore 0:
  10.9 44.6 all-reduce.9
  59.3 84.8 all-reduce.23
  323.7 121.4 all-reduce.11
  449.7 125.5 all-reduce.13
  579.9 125.5 all-reduce.15
  710.0 125.5 all-reduce.17
  840.3 125.5 all-reduce.19
  991.3 39.6 all-reduce.21
where the time goes:
time: 1050 us
  waiting for transfers between devices  798 us (76%)
  blocking collectives  212 us (20%)
  matrix products  19.9 us (2%)
  between operations  14.9 us (1%)
    psum x5, waiting for transfers between devices, spread_orthogonalize(): lax.psum(jnp.einsum('mdr,mds->mrs', current, current, precision=precision...  631 us
    psum x1, blocking collectives, spread_orthogonalize(): lax.psum(jnp.sum(ranged * ranged, axis=(1, 2)), ('shards', 'tensor'))  177 us
    unnamed x9, waiting for transfers between devices  84.5 us
    psum x1, waiting for transfers between devices, shards(): lax.psum(jnp.einsum('mdf,mdr->mfr', gradient_widened, projector, precisio...  45.4 us
    psum x1, waiting for transfers between devices, shards(): complete_rows = lax.psum(projected_slice, 'tensor')  37.8 us
    all_gather x1, blocking collectives, shards(): lax.all_gather(spread_orthogonalize(ranged), 'shards', axis=1, tiled=True)  22.4 us
  transfers between devices with their start and end apart: 8, of which 8 were waited for; matrix products, arithmetic and copies ran while one was open for 0% of the time, Pallas kernels for 0%

commit v1 on v0

--- a/solution.py
+++ b/solution.py
@@ -24,9 +24,12 @@
     squares = lax.psum(jnp.sum(ranged * ranged, axis=(1, 2)), ("shards", "tensor"))
     current = ranged / (jnp.sqrt(squares) + NORM_EPS)[:, None, None]
     for sweep_index in range(NS_STEPS):
-        gram_matrix = lax.psum(
-            jnp.einsum("mdr,mds->mrs", current, current, precision=precision_highest),
-            ("shards", "tensor"),
+        gram_matrix = jnp.sum(
+            lax.all_gather(
+                jnp.einsum("mdr,mds->mrs", current, current, precision=precision_highest),
+                ("shards", "tensor"),
+            ),
+            axis=0,
         )
         current = newton_step(current, gram_matrix)
     return current

time: 1050 us -> 1270 us (1.21)
  waiting for transfers between devices: 798 us -> 965 us
  other arithmetic: 3.08 us -> 62.7 us
    all_gather x0 -> x5, waiting for transfers between devices: none -> 795 us  [spread_orthogonalize(): lax.all_gather(jnp.einsum('mdr,mds->mrs', current, current, precision=pre...]
    psum x5 -> x0, waiting for transfers between devices: 631 us -> none  [spread_orthogonalize(): lax.psum(jnp.einsum('mdr,mds->mrs', current, current, precision=precision...]
    reduce_sum x0 -> x5, other arithmetic: none -> 59.6 us  [spread_orthogonalize(): jnp.sum(lax.all_gather(jnp.einsum('mdr,mds->mrs', current, current, preci...]
where the time goes in v1:
time: 1270 us
  waiting for transfers between devices  965 us (76%)
  blocking collectives  213 us (17%)
  other arithmetic  62.7 us (5%)
  between operations  15 us (1%)
  matrix products  14.9 us (1%)
    all_gather x5, waiting for transfers between devices, spread_orthogonalize(): lax.all_gather(jnp.einsum('mdr,mds->mrs', current, current, precision=pre...  795 us
    psum x1, blocking collectives, spread_orthogonalize(): lax.psum(jnp.sum(ranged * ranged, axis=(1, 2)), ('shards', 'tensor'))  177 us
    unnamed x9, waiting for transfers between devices  84.5 us
    reduce_sum x5, other arithmetic, spread_orthogonalize(): jnp.sum(lax.all_gather(jnp.einsum('mdr,mds->mrs', current, current, preci...  59.6 us
    psum x1, waiting for transfers between devices, shards(): lax.psum(jnp.einsum('mdf,mdr->mfr', gradient_widened, projector, precisio...  45.4 us
    psum x1, waiting for transfers between devices, shards(): complete_rows = lax.psum(projected_slice, 'tensor')  39.7 us
  transfers between devices with their start and end apart: 8, of which 8 were waited for; matrix products, arithmetic and copies ran while one was open for 0% of the time, Pallas kernels for 0%

profile of v1, /device:TPU:0, one launch (start us, length us, event | category | flops | bytes accessed | tf_op | source)
XLA Modules:
  0.0 1273.9 jit_solution(17376283760000438413)
XLA Ops:
  7.2 0.0 copy-start
  7.2 0.0 all-reduce.5.cloned.1.call-start
  7.2 0.9 copy-done
  8.2 1.9 fusion.14
  10.1 0.0 all-reduce.5.cloned.1.call-update
  10.1 0.0 all-reduce.9.cloned.1.call-start
  10.2 45.4 %all-reduce.5.cloned.1.call-done = f32[2,128,256]{2,1,0:T(8,128)} async-done(((f32[2,128,256]{2,1,0:T(8,128)}), f32[2,128,256]{2,1,0:T(8,128)}) %all-reduce.5.cloned.1.call-update) | async-done | bytes 262160 | tf_op jit(solution)/shard_map/psum | solution.py:52
  55.6 1.3 convolution_bitcast_fusion
  56.9 1.1 copy.17
  57.9 0.0 all-reduce.9.cloned.1.call-update
  57.9 0.0 all-gather.11.cloned.1.call-start
  58.0 1.2 dynamic-slice
  59.9 84.4 %all-reduce.9.cloned.1.call-done = f32[2,192,256]{2,0,1:T(2,128)} async-done(((f32[2,192,256]{2,0,1:T(2,128)}), f32[2,192,256]{2,0,1:T(2,128)}) %all-reduce.9.cloned.1.call-update) | async-done | bytes 393232
  144.2 0.9 multiply_reduce_fusion
  145.1 176.9 %psum.22 = f32[2]{0:T(128)S(1)} all-reduce(f32[2]{0:T(128)S(1)} %get-tuple-element.20), channel_id=1, replica_groups=mesh['shards'=16,'tensor'=4,'section'=2] {'shards','tensor'}, use_global_device_ids=true, to_apply=%region_3.0 | all-reduce | flops 2 | bytes 16 | tf_op jit(solution)/shard_map/psum | solution.py:24
  322.0 1.5 fusion.10
  323.6 0.0 all-gather.11.cloned.1.call-update
  323.6 0.0 all-gather.13.cloned.1.call-start
  323.6 154.0 %all-gather.11.cloned.1.call-done = f32[128,256,256]{2,1,0:T(8,128)} async-done(((f32[2,256,256]{2,1,0:T(8,128)}), f32[128,256,256]{2,1,0:T(8,128)}) %all-gather.11.cloned.1.call-update) | async-done | bytes 33554448 | tf_op jit(solution)/shard_map/all_gather | solution.py:28
  477.7 11.9 reduce_sum.55
  489.6 0.4 fusion.8
  490.0 1.4 fusion.15
  491.4 0.0 all-gather.13.cloned.1.call-update
  491.4 0.0 all-gather.15.cloned.1.call-start
  491.5 160.3 %all-gather.13.cloned.1.call-done = f32[128,256,256]{2,1,0:T(8,128)} async-done(((f32[2,256,256]{2,1,0:T(8,128)}), f32[128,256,256]{2,1,0:T(8,128)}) %all-gather.13.cloned.1.call-update) | async-done | bytes 33554448 | tf_op jit(solution)/shard_map/all_gather | solution.py:28
  651.7 11.9 reduce_sum.56
  663.6 0.4 fusion.7
  664.0 1.5 fusion.16
  665.5 0.0 all-gather.15.cloned.1.call-update
  665.5 0.0 all-gather.17.cloned.1.call-start
  665.5 160.2 %all-gather.15.cloned.1.call-done = f32[128,256,256]{2,1,0:T(8,128)} async-done(((f32[2,256,256]{2,1,0:T(8,128)}), f32[128,256,256]{2,1,0:T(8,128)}) %all-gather.15.cloned.1.call-update) | async-done | bytes 33554448 | tf_op jit(solution)/shard_map/all_gather | solution.py:28
  825.8 11.9 reduce_sum.57
  837.7 0.4 fusion.6
  838.0 1.5 fusion.17
  839.5 0.0 all-gather.17.cloned.1.call-update
  839.5 0.0 all-gather.19.cloned.1.call-start
  839.6 160.2 %all-gather.17.cloned.1.call-done = f32[128,256,256]{2,1,0:T(8,128)} async-done(((f32[2,256,256]{2,1,0:T(8,128)}), f32[128,256,256]{2,1,0:T(8,128)}) %all-gather.17.cloned.1.call-update) | async-done | bytes 33554448 | tf_op jit(solution)/shard_map/all_gather | solution.py:28
  999.8 0.0 copy-start.9
  999.8 0.0 copy-start.10
  999.9 0.0 copy-start.5
  999.9 0.0 copy-start.6
  999.9 0.0 copy-start.4
  999.9 12.0 reduce_sum.58
  1011.9 0.4 fusion.5
  1012.3 1.5 fusion.18
  1013.7 0.0 all-gather.19.cloned.1.call-update
  1013.8 0.0 all-reduce.7.cloned.1.call-start
  1013.8 160.2 %all-gather.19.cloned.1.call-done = f32[128,256,256]{2,1,0:T(8,128)} async-done(((f32[2,256,256]{2,1,0:T(8,128)}), f32[128,256,256]{2,1,0:T(8,128)}) %all-gather.19.cloned.1.call-update) | async-done | bytes 33554448 | tf_op jit(solution)/shard_map/all_gather | solution.py:28
  1174.1 11.9 reduce_sum.59
  1186.0 0.4 fusion.4
  1186.4 23.9 %all_gather.46 = f32[2,192,256]{2,0,1:T(2,128)S(1)} all-gather(f32[2,12,256]{2,0,1:T(2,128)S(1)} %copy.19), channel_id=1, replica_groups=mesh['shards'=16,'tensor'=4,'section'=2] {'shards'}, dimensions={1}, use_global_device_ids=true | all-gather | bytes 417792 | tf_op jit(solution)/shard_map/all_gather | solution.py:58
  1210.3 0.0 copy-done.3
  1210.3 0.0 copy-start.2
  1210.3 1.4 fusion.19
  1211.6 0.0 all-reduce.7.cloned.1.call-update
  1211.7 0.0 copy-done.11
  1211.7 0.0 copy-done.7
  1211.7 0.7 divide_subtract_fusion
  1212.4 39.7 %all-reduce.7.cloned.1.call-done = f32[2,256,128]{2,1,0:T(8,128)} async-done(((f32[2,256,128]{2,1,0:T(8,128)}), f32[2,256,128]{2,1,0:T(8,128)}) %all-reduce.7.cloned.1.call-update) | async-done | bytes 262160 | tf_op jit(solution)/shard_map/psum | solution.py:63
  1252.1 0.0 copy-done.6
  1252.1 1.5 multiply_divide_fusion
  1253.7 12.2 all_gather.47
  1265.9 1.2 fusion.3
  1267.1 0.0 copy-done.1
  (15 shorter events, 0.1 us)
Async XLA Ops:
  7.2 1.0 copy-start
  7.2 48.4 %all-reduce.5.cloned.1.call-start = ((), (), s32[]{:S(2)}) async-start(), calls=%async_computation | async-start | bytes 524288 | tf_op jit(solution)/shard_map/psum | solution.py:52
  10.1 134.1 %all-reduce.9.cloned.1.call-start = ((), (), s32[]{:S(2)}) async-start(), calls=%async_computation.7 | async-start | bytes 786432
  57.9 419.7 %all-gather.11.cloned.1.call-start = ((), (), s32[]{:S(2)}) async-start(), calls=%async_computation.2 | async-start | bytes 34078720 | tf_op jit(solution)/shard_map/all_gather | solution.py:28
  323.6 328.1 %all-gather.13.cloned.1.call-start = ((), (), s32[]{:S(2)}) async-start(), calls=%async_computation.3 | async-start | bytes 34078720 | tf_op jit(solution)/shard_map/all_gather | solution.py:28
  491.4 334.4 %all-gather.15.cloned.1.call-start = ((), (), s32[]{:S(2)}) async-start(), calls=%async_computation.4 | async-start | bytes 34078720 | tf_op jit(solution)/shard_map/all_gather | solution.py:28
  665.5 334.3 %all-gather.17.cloned.1.call-start = ((), (), s32[]{:S(2)}) async-start(), calls=%async_computation.5 | async-start | bytes 34078720 | tf_op jit(solution)/shard_map/all_gather | solution.py:28
  839.5 334.5 %all-gather.19.cloned.1.call-start = ((), (), s32[]{:S(2)}) async-start(), calls=%async_computation.6 | async-start | bytes 34078720 | tf_op jit(solution)/shard_map/all_gather | solution.py:28
  999.8 267.2 %copy-start.1 = (f32[2,192,256]{2,1,0:T(8,128)S(1)}, f32[2,192,256]{2,1,0:T(8,128)}, u32[]{:S(2)}) copy-start(f32[2,192,256]{2,1,0:T(8,128)} %param.12) | copy-start | bytes 1179652
  999.8 210.4 %copy-start.3 = (bf16[2,192,128]{2,1,0:T(8,128)(2,1)S(1)}, bf16[2,192,128]{2,1,0:T(8,128)(2,1)}, u32[]{:S(2)}) copy-start(bf16[2,192,128]{2,1,0:T(8,128)(2,1)} %param.10) | copy-start | bytes 294916
  999.8 211.8 %copy-start.11 = (s32[2]{0:T(128)S(1)}, s32[2]{0:T(128)}, u32[]{:S(2)}) copy-start(s32[2]{0:T(128)} %param.15) | copy-start | bytes 28
  999.8 211.9 %copy-start.7 = (f32[2,192]{1,0:T(2,128)S(1)}, f32[2,192]{1,0:T(2,128)}, u32[]{:S(2)}) copy-start(f32[2,192]{1,0:T(2,128)} %param.16) | copy-start | bytes 4612
  999.8 211.9 %copy-start.8 = (f32[2,192]{1,0:T(2,128)S(1)}, f32[2,192]{1,0:T(2,128)}, u32[]{:S(2)}) copy-start(f32[2,192]{1,0:T(2,128)} %param.17) | copy-start | bytes 4612
  999.8 211.9 %copy-start.9 = (f32[2,192]{1,0:T(2,128)S(1)}, f32[2,192]{1,0:T(2,128)}, u32[]{:S(2)}) copy-start(f32[2,192]{1,0:T(2,128)} %param.18) | copy-start | bytes 4612
  999.8 211.9 %copy-start.10 = (f32[2,192]{1,0:T(2,128)S(1)}, f32[2,192]{1,0:T(2,128)}, u32[]{:S(2)}) copy-start(f32[2,192]{1,0:T(2,128)} %param.19) | copy-start | bytes 4612
  999.9 252.3 %copy-start.5 = (f32[2,64,128]{2,1,0:T(8,128)S(1)}, f32[2,64,128]{2,1,0:T(8,128)}, u32[]{:S(2)}) copy-start(f32[2,64,128]{2,1,0:T(8,128)} %param.14) | copy-start | bytes 196612
  999.9 252.3 %copy-start.6 = (f32[2,64,128]{2,1,0:T(8,128)S(1)}, f32[2,64,128]{2,1,0:T(8,128)}, u32[]{:S(2)}) copy-start(f32[2,64,128]{2,1,0:T(8,128)} %param.13) | copy-start | bytes 196612
  999.9 266.0 %copy-start.4 = (bf16[2,192,128]{2,1,0:T(8,128)(2,1)S(1)}, bf16[2,192,128]{2,1,0:T(8,128)(2,1)}, u32[]{:S(2)}) copy-start(bf16[2,192,128]{2,1,0:T(8,128)(2,1)} %param.11) | copy-start | bytes 294916
  1013.8 238.4 %all-reduce.7.cloned.1.call-start = ((), (), s32[]{:S(2)}) async-start(), calls=%async_computation.1 | async-start | bytes 524288 | tf_op jit(solution)/shard_map/psum | solution.py:63
  1210.3 56.8 %copy-start.2 = (f32[2,192,256]{2,1,0:T(8,128)}, f32[2,192,256]{2,1,0:T(8,128)S(1)}, u32[]{:S(2)}) copy-start(f32[2,192,256]{2,1,0:T(8,128)S(1)} %copy.21) | copy-start | bytes 1179652
Sparse Core Ops, SparseCore 0:
  10.9 44.6 all-reduce.4
  59.3 84.8 all-reduce.8
  323.7 153.9 all-gather.10
  491.5 160.1 all-gather.12
  665.6 160.1 all-gather.14
  839.6 160.1 all-gather.16
  1013.9 160.1 all-gather.18
  1211.8 40.2 all-reduce.6
